TPU v7x, 256 devices: a whole 4x4x8 slice. The times are simulated.
256 devices in a mesh: row: 16 (over z_hi, y), col: 16 (over z_lo, x, core).
Axes of the slice: x: 4, y: 4, z: 8 (z_hi: 4, z_lo: 2; z = z_hi * 2 + z_lo), core: 2. Of those that a mesh axis runs over, the one named last changes fastest.
Arguments:
- right_side: float32 [16, 16, 1024, 256], P('row', 'col'), may hold values from -4 to 4
- local_operator: bfloat16 [16, 16, 1536, 1536], P('row', 'col'), may hold values from -1 to 4
- local_inverse: bfloat16 [16, 16, 1536, 1536], P('row', 'col'), may hold values from -1 to 1
- coarse_basis: bfloat16 [16, 16, 1536, 32], P('row', 'col'), may hold values from -1 to 1
- coarse_inverse: bfloat16 [16, 512, 8192], P(None, 'col', 'row'), may hold values from -1 to 1
- send_rows: int32 [16, 16, 4, 128], P('row', 'col'), may hold values from 0 to 1023, as said below
- send_count: int32 [16, 16, 4], P('row', 'col'), may hold values from 0 to 128, as said below
Outputs:
- solution: float32 [16, 16, 1024, 256], P('row', 'col')
Inputs may be any that keep to these rules, and one draw needn't show every extreme that they name: `send_rows`: within one subdomain and direction the entries are distinct owned rows; entries at or past that direction's count are ignored. `send_count`: 0 exactly where the neighbour in that direction lies outside the grid of subdomains; otherwise from 128 // 4 to 128, and 128 is reached.
All inputs are finite; a program needn't handle non-finite values.
Results may differ from a plain program's by a relative error of at most 0.023.
Values may be sent and summed in bfloat16 or wider, within the bound.
A program may use at most 64 MiB of HBM per device.

v0:
```python
import jax
import jax.numpy as jnp
from jax import lax
from jax.sharding import PartitionSpec as P

ITERS = 3
DAMPING = 0.5


def passed_along(shard, axis, by):
    devices = lax.axis_size(axis)
    pairs = [(i, i + by) for i in range(devices) if 0 <= i + by < devices]
    return lax.ppermute(shard, axis, pairs)


def ghost_trade(buffer):
    arrived = []
    for offset, source in ((1, 1), (-1, 0)):
        arrived.append(passed_along(buffer[source], "row", offset))
    for offset, source in ((1, 3), (-1, 2)):
        arrived.append(passed_along(buffer[source], "col", offset))
    return jnp.stack(arrived)


def per_device(
    right_side, local_operator, local_inverse, coarse_basis, coarse_inverse, send_rows, send_count
):
    target = right_side[0, 0]
    operator = local_operator[0, 0]
    inverse = local_inverse[0, 0]
    prolong = coarse_basis[0, 0]
    rows_list = send_rows[0, 0]
    counts = send_count[0, 0]
    own_rows, columns = target.shape
    tile_rows = rows_list.shape[1]
    live_mask = (lax.broadcasted_iota(jnp.int32, rows_list.shape, 1) < counts[:, None]).astype(
        jnp.float32
    )
    live_half = live_mask[..., None].astype(jnp.bfloat16)
    flat_rows = rows_list.reshape(-1)
    coarse_rows = coarse_inverse.reshape(-1, coarse_inverse.shape[2])

    def with_ghosts(values_half):
        packed = values_half[flat_rows].reshape(4, tile_rows, columns) * live_half
        ghosts = ghost_trade(packed)
        return jnp.concatenate([values_half, ghosts.reshape(4 * tile_rows, columns)], axis=0)

    def owner_sum(local_terms):
        rim_half = local_terms[own_rows:].astype(jnp.bfloat16).reshape(4, tile_rows, columns)
        returned = ghost_trade(rim_half)
        weighted = returned.astype(jnp.float32) * live_mask[..., None]
        summed = (
            jnp.zeros((own_rows, columns), jnp.float32)
            .at[flat_rows]
            .add(weighted.reshape(-1, columns))
        )
        return local_terms[:own_rows] + summed

    solution = jnp.zeros((own_rows, columns), jnp.float32)
    for sweep in range(ITERS):
        if sweep == 0:
            residual_half = target.astype(jnp.bfloat16)
        else:
            solution_half = solution.astype(jnp.bfloat16)
            image = owner_sum(
                jnp.dot(operator, with_ghosts(solution_half), preferred_element_type=jnp.float32)
            )
            residual_half = (target - image).astype(jnp.bfloat16)
        residual_local = with_ghosts(residual_half)
        local_part = jnp.dot(inverse, residual_local, preferred_element_type=jnp.float32)
        restricted = lax.dot_general(
            prolong, residual_local, (((0,), (0,)), ((), ())), preferred_element_type=jnp.float32
        )
        restricted = restricted.astype(jnp.bfloat16)
        block_rows = lax.all_gather(restricted, "col", axis=0, tiled=True)
        solved = lax.psum_scatter(
            jnp.dot(coarse_rows, block_rows, preferred_element_type=jnp.float32).astype(
                jnp.bfloat16
            ),
            "row",
            scatter_dimension=0,
            tiled=True,
        )
        update = owner_sum(
            local_part + jnp.dot(prolong, solved, preferred_element_type=jnp.float32)
        )
        solution = solution + DAMPING * update
    return solution[None, None]


def solution(mesh):
    return jax.shard_map(
        per_device,
        mesh=mesh,
        in_specs=(
            P("row", "col", None, None),
            P("row", "col", None, None),
            P("row", "col", None, None),
            P("row", "col", None, None),
            P(None, "col", "row"),
            P("row", "col", None, None),
            P("row", "col", None),
        ),
        out_specs=P("row", "col", None, None),
        check_vma=False,
    )
```

profile of v0, /device:TPU:89, one launch (start us, length us, event | category | flops | bytes accessed | tf_op | source)
XLA Modules:
  0.0 582.0 jit_solution(5471875140377850859)
XLA Ops:
  11.4 5.8 collective-permute-start
  20.1 3.0 collective-permute-start.2
  25.1 8.6 %collective-permute-done.1 = bf16[128,256]{1,0:T(8,128)(2,1)S(1)} collective-permute-done((bf16[128,256]{1,0:T(8,128)(2,1)S(1)}, bf16[128,256]{1,0:T(8,128)(2,1)S(1)}, u32[]{:S(2)}, u32[]{:S(2)}) %collective-permute-start.1) | collective-permute-done | bytes 65568 | tf_op jit(solution)/shard_map/ppermute | solution.py:13
  33.9 19.0 %all_gather.9 = bf16[512,256]{1,0:T(8,128)(2,1)S(1)} all-gather(bf16[32,256]{1,0:T(8,128)(2,1)S(1)} %fusion.22), channel_id=1, replica_groups=mesh['row'=16,'col'=16] {'col'}, dimensions={0}, use_global_device_ids=true | all-gather | bytes 278528 | tf_op jit(solution)/shard_map/all_gather | solution.py:75
  54.3 3.8 fusion.8
  58.0 75.6 %reduce-scatter.10.cloned.1.call-done = bf16[32,256]{1,0:T(8,128)(2,1)} async-done(((bf16[512,256]{1,0:T(8,128)(2,1)}), bf16[32,256]{1,0:T(8,128)(2,1)}) %reduce-scatter.10.cloned.1.call-update) | async-done | bytes 16400
  134.8 4.5 collective-permute-start.4
  139.3 5.0 collective-permute-start.7
  144.3 3.0 collective-permute-start.6
  149.7 9.0 %collective-permute-done.5 = bf16[128,256]{0,1:T(8,128)(2,1)S(1)} collective-permute-done((bf16[128,256]{0,1:T(8,128)(2,1)S(1)}, bf16[128,256]{0,1:T(8,128)(2,1)S(1)}, u32[]{:S(2)}, u32[]{:S(2)}) %collective-permute-start.5) | collective-permute-done | bytes 65568 | tf_op jit(solution)/shard_map/ppermute | solution.py:13
  159.1 3.7 scatter_fusion
  169.3 3.3 collective-permute-start.10
  172.5 3.4 collective-permute-start.9
  175.9 7.6 %collective-permute-done.9 = bf16[128,256]{1,0:T(8,128)(2,1)S(1)} collective-permute-done((bf16[128,256]{1,0:T(8,128)(2,1)S(1)}, bf16[128,256]{1,0:T(8,128)(2,1)S(1)}, u32[]{:S(2)}, u32[]{:S(2)}) %collective-permute-start.9) | collective-permute-done | bytes 65568 | tf_op jit(solution)/shard_map/ppermute | solution.py:13
  183.5 3.8 fusion.54
  191.2 3.6 collective-permute-start.14
  194.9 3.4 collective-permute-start.13
  200.9 3.4 collective-permute-done.13
  206.5 3.9 scatter_fusion.1
  218.6 3.6 collective-permute-start.18
  222.3 3.1 collective-permute-start.17
  225.4 6.8 %collective-permute-done.17 = bf16[128,256]{1,0:T(8,128)(2,1)S(1)} collective-permute-done((bf16[128,256]{1,0:T(8,128)(2,1)S(1)}, bf16[128,256]{1,0:T(8,128)(2,1)S(1)}, u32[]{:S(2)}, u32[]{:S(2)}) %collective-permute-start.17) | collective-permute-done | bytes 65568 | tf_op jit(solution)/shard_map/ppermute | solution.py:13
  232.5 18.0 %all_gather.10 = bf16[512,256]{1,0:T(8,128)(2,1)S(1)} all-gather(bf16[32,256]{1,0:T(8,128)(2,1)S(1)} %fusion.23), channel_id=1, replica_groups=mesh['row'=16,'col'=16] {'col'}, dimensions={0}, use_global_device_ids=true | all-gather | bytes 278528 | tf_op jit(solution)/shard_map/all_gather | solution.py:75
  251.7 5.0 fusion.6
  256.7 77.3 %reduce-scatter.12.cloned.1.call-done = bf16[32,256]{1,0:T(8,128)(2,1)} async-done(((bf16[512,256]{1,0:T(8,128)(2,1)}), bf16[32,256]{1,0:T(8,128)(2,1)}) %reduce-scatter.12.cloned.1.call-update) | async-done | bytes 16400
  335.8 4.5 collective-permute-start.20
  340.3 5.0 collective-permute-start.23
  345.3 3.0 collective-permute-start.22
  352.9 6.8 %collective-permute-done.21 = bf16[128,256]{0,1:T(8,128)(2,1)S(1)} collective-permute-done((bf16[128,256]{0,1:T(8,128)(2,1)S(1)}, bf16[128,256]{0,1:T(8,128)(2,1)S(1)}, u32[]{:S(2)}, u32[]{:S(2)}) %collective-permute-start.21) | collective-permute-done | bytes 65568 | tf_op jit(solution)/shard_map/ppermute | solution.py:13
  361.9 3.7 scatter_fusion.2
  372.2 3.3 collective-permute-start.26
  375.4 3.4 collective-permute-start.25
  378.8 7.6 %collective-permute-done.25 = bf16[128,256]{1,0:T(8,128)(2,1)S(1)} collective-permute-done((bf16[128,256]{1,0:T(8,128)(2,1)S(1)}, bf16[128,256]{1,0:T(8,128)(2,1)S(1)}, u32[]{:S(2)}, u32[]{:S(2)}) %collective-permute-start.25) | collective-permute-done | bytes 65568 | tf_op jit(solution)/shard_map/ppermute | solution.py:13
  386.4 3.8 fusion.56
  394.3 3.6 collective-permute-start.30
  398.0 3.4 collective-permute-start.29
  409.6 5.2 scatter_fusion.3
  418.6 3.8 collective-permute-start.32
  424.3 3.6 collective-permute-start.34
  429.9 8.0 %collective-permute-done.33 = bf16[128,256]{1,0:T(8,128)(2,1)S(1)} collective-permute-done((bf16[128,256]{1,0:T(8,128)(2,1)S(1)}, bf16[128,256]{1,0:T(8,128)(2,1)S(1)}, u32[]{:S(2)}, u32[]{:S(2)}) %collective-permute-start.33) | collective-permute-done | bytes 65568 | tf_op jit(solution)/shard_map/ppermute | solution.py:13
  438.6 17.8 %all_gather.11 = bf16[512,256]{1,0:T(8,128)(2,1)S(1)} all-gather(bf16[32,256]{1,0:T(8,128)(2,1)S(1)} %fusion.24), channel_id=1, replica_groups=mesh['row'=16,'col'=16] {'col'}, dimensions={0}, use_global_device_ids=true | all-gather | bytes 278528 | tf_op jit(solution)/shard_map/all_gather | solution.py:75
  457.7 5.0 fusion.4
  462.7 77.3 %reduce-scatter.14.cloned.1.call-done = bf16[32,256]{1,0:T(8,128)(2,1)} async-done(((bf16[512,256]{1,0:T(8,128)(2,1)}), bf16[32,256]{1,0:T(8,128)(2,1)}) %reduce-scatter.14.cloned.1.call-update) | async-done | bytes 16400
  541.9 4.5 collective-permute-start.36
  546.4 5.0 collective-permute-start.39
  551.4 3.0 collective-permute-start.38
  560.0 5.7 collective-permute-done.37
  567.8 5.2 scatter_fusion.4
  (131 shorter events, 88.9 us)
Async XLA Ops:
  6.5 46.5 %copy-start = (bf16[16,32,512]{2,1,0:T(8,128)(2,1)S(1)}, bf16[16,32,512]{2,1,0:T(8,128)(2,1)}, u32[]{:S(2)}) copy-start(bf16[16,32,512]{2,1,0:T(8,128)(2,1)} %param.11) | copy-start | bytes 1572868
  6.5 127.1 %reduce-scatter.10.cloned.1.call-start = ((), (), s32[]{:S(2)}) async-start(), calls=%async_computation.3 | async-start | bytes 278528
  9.3 24.4 %copy-start.1 = (bf16[1,1,1536,32]{2,3,1,0:T(8,128)(2,1)S(1)}, bf16[1,1,1536,32]{2,3,1,0:T(8,128)(2,1)}, u32[]{:S(2)}) copy-start(bf16[1,1,1536,32]{2,3,1,0:T(8,128)(2,1)} %param.10) | copy-start | bytes 294916
  11.4 13.6 %collective-permute-start = (bf16[128,256]{1,0:T(8,128)(2,1)S(1)}, bf16[128,256]{1,0:T(8,128)(2,1)S(1)}, u32[]{:S(2)}, u32[]{:S(2)}) collective-permute-start(bf16[128,256]{1,0:T(8,128)(2,1)S(1)} %get-tuple-element.41), channel_id=1, source_target_pairs={{0,16},{16,32},{32,48},{48,64},{64,80},{80,96},{96,112},{112,128},... | collective-permute-start | bytes 196616 | tf_op jit(solution)/shard_map/ppermute | solution.py:13
  17.2 7.8 %collective-permute-start.3 = (bf16[128,256]{1,0:T(8,128)(2,1)S(1)}, bf16[128,256]{1,0:T(8,128)(2,1)S(1)}, u32[]{:S(2)}, u32[]{:S(2)}) collective-permute-start(bf16[128,256]{1,0:T(8,128)(2,1)S(1)} %get-tuple-element.42), channel_id=1, source_target_pairs={{1,0},{2,1},{3,2},{4,3},{5,4},{6,5},{7,6},{8,7},{9,8},{10,9},{11,1... | collective-permute-start | bytes 196616 | tf_op jit(solution)/shard_map/ppermute | solution.py:13
  20.1 5.0 collective-permute-start.2
  23.1 10.5 %collective-permute-start.1 = (bf16[128,256]{1,0:T(8,128)(2,1)S(1)}, bf16[128,256]{1,0:T(8,128)(2,1)S(1)}, u32[]{:S(2)}, u32[]{:S(2)}) collective-permute-start(bf16[128,256]{1,0:T(8,128)(2,1)S(1)} %get-tuple-element.44), channel_id=1, source_target_pairs={{16,0},{32,16},{48,32},{64,48},{80,64},{96,80},{112,96},{128,112},... | collective-permute-start | bytes 196616 | tf_op jit(solution)/shard_map/ppermute | solution.py:13
  54.2 279.7 %reduce-scatter.12.cloned.1.call-start = ((), (), s32[]{:S(2)}) async-start(), calls=%async_computation.4 | async-start | bytes 278528
  134.8 14.8 %collective-permute-start.4 = (bf16[128,256]{0,1:T(8,128)(2,1)S(1)}, bf16[128,256]{0,1:T(8,128)(2,1)S(1)}, u32[]{:S(2)}, u32[]{:S(2)}) collective-permute-start(bf16[128,256]{0,1:T(8,128)(2,1)S(1)} %get-tuple-element.21), channel_id=1, source_target_pairs={{0,16},{16,32},{32,48},{48,64},{64,80},{80,96},{96,112},{112,128},... | collective-permute-start | bytes 196616 | tf_op jit(solution)/shard_map/ppermute | solution.py:13
  139.3 10.4 %collective-permute-start.7 = (bf16[128,256]{0,1:T(8,128)(2,1)S(1)}, bf16[128,256]{0,1:T(8,128)(2,1)S(1)}, u32[]{:S(2)}, u32[]{:S(2)}) collective-permute-start(bf16[128,256]{0,1:T(8,128)(2,1)S(1)} %get-tuple-element.22), channel_id=1, source_target_pairs={{1,0},{2,1},{3,2},{4,3},{5,4},{6,5},{7,6},{8,7},{9,8},{10,9},{11,1... | collective-permute-start | bytes 196616 | tf_op jit(solution)/shard_map/ppermute | solution.py:13
  144.3 5.4 collective-permute-start.6
  147.3 11.4 %collective-permute-start.5 = (bf16[128,256]{0,1:T(8,128)(2,1)S(1)}, bf16[128,256]{0,1:T(8,128)(2,1)S(1)}, u32[]{:S(2)}, u32[]{:S(2)}) collective-permute-start(bf16[128,256]{0,1:T(8,128)(2,1)S(1)} %get-tuple-element.24), channel_id=1, source_target_pairs={{16,0},{32,16},{48,32},{64,48},{80,64},{96,80},{112,96},{128,112},... | collective-permute-start | bytes 196616 | tf_op jit(solution)/shard_map/ppermute | solution.py:13
  165.0 10.9 %collective-permute-start.8 = (bf16[128,256]{1,0:T(8,128)(2,1)S(1)}, bf16[128,256]{1,0:T(8,128)(2,1)S(1)}, u32[]{:S(2)}, u32[]{:S(2)}) collective-permute-start(bf16[128,256]{1,0:T(8,128)(2,1)S(1)} %get-tuple-element.37), channel_id=1, source_target_pairs={{0,16},{16,32},{32,48},{48,64},{64,80},{80,96},{96,112},{112,128},... | collective-permute-start | bytes 196616 | tf_op jit(solution)/shard_map/ppermute | solution.py:13
  166.9 9.0 %collective-permute-start.11 = (bf16[128,256]{1,0:T(8,128)(2,1)S(1)}, bf16[128,256]{1,0:T(8,128)(2,1)S(1)}, u32[]{:S(2)}, u32[]{:S(2)}) collective-permute-start(bf16[128,256]{1,0:T(8,128)(2,1)S(1)} %get-tuple-element.38), channel_id=1, source_target_pairs={{1,0},{2,1},{3,2},{4,3},{5,4},{6,5},{7,6},{8,7},{9,8},{10,9},{11,1... | collective-permute-start | bytes 196616 | tf_op jit(solution)/shard_map/ppermute | solution.py:13
  169.3 6.7 %collective-permute-start.10 = (bf16[128,256]{1,0:T(8,128)(2,1)S(1)}, bf16[128,256]{1,0:T(8,128)(2,1)S(1)}, u32[]{:S(2)}, u32[]{:S(2)}) collective-permute-start(bf16[128,256]{1,0:T(8,128)(2,1)S(1)} %get-tuple-element.39), channel_id=1, source_target_pairs={{0,1},{1,2},{2,3},{3,4},{4,5},{5,6},{6,7},{7,8},{8,9},{9,10},{10,1... | collective-permute-start | bytes 196616 | tf_op jit(solution)/shard_map/ppermute | solution.py:13
  172.5 11.0 %collective-permute-start.9 = (bf16[128,256]{1,0:T(8,128)(2,1)S(1)}, bf16[128,256]{1,0:T(8,128)(2,1)S(1)}, u32[]{:S(2)}, u32[]{:S(2)}) collective-permute-start(bf16[128,256]{1,0:T(8,128)(2,1)S(1)} %get-tuple-element.40), channel_id=1, source_target_pairs={{16,0},{32,16},{48,32},{64,48},{80,64},{96,80},{112,96},{128,112},... | collective-permute-start | bytes 196616 | tf_op jit(solution)/shard_map/ppermute | solution.py:13
  187.4 13.5 %collective-permute-start.12 = (bf16[128,256]{0,1:T(8,128)(2,1)S(1)}, bf16[128,256]{0,1:T(8,128)(2,1)S(1)}, u32[]{:S(2)}, u32[]{:S(2)}) collective-permute-start(bf16[128,256]{0,1:T(8,128)(2,1)S(1)} %get-tuple-element.17), channel_id=1, source_target_pairs={{0,16},{16,32},{32,48},{48,64},{64,80},{80,96},{96,112},{112,128},... | collective-permute-start | bytes 196616 | tf_op jit(solution)/shard_map/ppermute | solution.py:13
  189.3 11.6 %collective-permute-start.15 = (bf16[128,256]{0,1:T(8,128)(2,1)S(1)}, bf16[128,256]{0,1:T(8,128)(2,1)S(1)}, u32[]{:S(2)}, u32[]{:S(2)}) collective-permute-start(bf16[128,256]{0,1:T(8,128)(2,1)S(1)} %get-tuple-element.18), channel_id=1, source_target_pairs={{1,0},{2,1},{3,2},{4,3},{5,4},{6,5},{7,6},{8,7},{9,8},{10,9},{11,1... | collective-permute-start | bytes 196616 | tf_op jit(solution)/shard_map/ppermute | solution.py:13
  191.2 9.7 %collective-permute-start.14 = (bf16[128,256]{0,1:T(8,128)(2,1)S(1)}, bf16[128,256]{0,1:T(8,128)(2,1)S(1)}, u32[]{:S(2)}, u32[]{:S(2)}) collective-permute-start(bf16[128,256]{0,1:T(8,128)(2,1)S(1)} %get-tuple-element.19), channel_id=1, source_target_pairs={{0,1},{1,2},{2,3},{3,4},{4,5},{5,6},{6,7},{7,8},{8,9},{9,10},{10,1... | collective-permute-start | bytes 196616 | tf_op jit(solution)/shard_map/ppermute | solution.py:13
  194.9 9.4 %collective-permute-start.13 = (bf16[128,256]{0,1:T(8,128)(2,1)S(1)}, bf16[128,256]{0,1:T(8,128)(2,1)S(1)}, u32[]{:S(2)}, u32[]{:S(2)}) collective-permute-start(bf16[128,256]{0,1:T(8,128)(2,1)S(1)} %get-tuple-element.20), channel_id=1, source_target_pairs={{16,0},{32,16},{48,32},{64,48},{80,64},{96,80},{112,96},{128,112},... | collective-permute-start | bytes 196616 | tf_op jit(solution)/shard_map/ppermute | solution.py:13
  213.9 11.4 %collective-permute-start.16 = (bf16[128,256]{1,0:T(8,128)(2,1)S(1)}, bf16[128,256]{1,0:T(8,128)(2,1)S(1)}, u32[]{:S(2)}, u32[]{:S(2)}) collective-permute-start(bf16[128,256]{1,0:T(8,128)(2,1)S(1)} %get-tuple-element.33), channel_id=1, source_target_pairs={{0,16},{16,32},{32,48},{48,64},{64,80},{80,96},{96,112},{112,128},... | collective-permute-start | bytes 196616 | tf_op jit(solution)/shard_map/ppermute | solution.py:13
  216.7 8.7 %collective-permute-start.19 = (bf16[128,256]{1,0:T(8,128)(2,1)S(1)}, bf16[128,256]{1,0:T(8,128)(2,1)S(1)}, u32[]{:S(2)}, u32[]{:S(2)}) collective-permute-start(bf16[128,256]{1,0:T(8,128)(2,1)S(1)} %get-tuple-element.34), channel_id=1, source_target_pairs={{1,0},{2,1},{3,2},{4,3},{5,4},{6,5},{7,6},{8,7},{9,8},{10,9},{11,1... | collective-permute-start | bytes 196616 | tf_op jit(solution)/shard_map/ppermute | solution.py:13
  218.6 6.7 %collective-permute-start.18 = (bf16[128,256]{1,0:T(8,128)(2,1)S(1)}, bf16[128,256]{1,0:T(8,128)(2,1)S(1)}, u32[]{:S(2)}, u32[]{:S(2)}) collective-permute-start(bf16[128,256]{1,0:T(8,128)(2,1)S(1)} %get-tuple-element.35), channel_id=1, source_target_pairs={{0,1},{1,2},{2,3},{3,4},{4,5},{5,6},{6,7},{7,8},{8,9},{9,10},{10,1... | collective-permute-start | bytes 196616 | tf_op jit(solution)/shard_map/ppermute | solution.py:13
  222.3 9.9 %collective-permute-start.17 = (bf16[128,256]{1,0:T(8,128)(2,1)S(1)}, bf16[128,256]{1,0:T(8,128)(2,1)S(1)}, u32[]{:S(2)}, u32[]{:S(2)}) collective-permute-start(bf16[128,256]{1,0:T(8,128)(2,1)S(1)} %get-tuple-element.36), channel_id=1, source_target_pairs={{16,0},{32,16},{48,32},{64,48},{80,64},{96,80},{112,96},{128,112},... | collective-permute-start | bytes 196616 | tf_op jit(solution)/shard_map/ppermute | solution.py:13
  251.7 288.4 %reduce-scatter.14.cloned.1.call-start = ((), (), s32[]{:S(2)}) async-start(), calls=%async_computation.5 | async-start | bytes 278528
  335.8 17.1 %collective-permute-start.20 = (bf16[128,256]{0,1:T(8,128)(2,1)S(1)}, bf16[128,256]{0,1:T(8,128)(2,1)S(1)}, u32[]{:S(2)}, u32[]{:S(2)}) collective-permute-start(bf16[128,256]{0,1:T(8,128)(2,1)S(1)} %get-tuple-element.13), channel_id=1, source_target_pairs={{0,16},{16,32},{32,48},{48,64},{64,80},{80,96},{96,112},{112,128},... | collective-permute-start | bytes 196616 | tf_op jit(solution)/shard_map/ppermute | solution.py:13
  340.3 12.6 %collective-permute-start.23 = (bf16[128,256]{0,1:T(8,128)(2,1)S(1)}, bf16[128,256]{0,1:T(8,128)(2,1)S(1)}, u32[]{:S(2)}, u32[]{:S(2)}) collective-permute-start(bf16[128,256]{0,1:T(8,128)(2,1)S(1)} %get-tuple-element.14), channel_id=1, source_target_pairs={{1,0},{2,1},{3,2},{4,3},{5,4},{6,5},{7,6},{8,7},{9,8},{10,9},{11,1... | collective-permute-start | bytes 196616 | tf_op jit(solution)/shard_map/ppermute | solution.py:13
  345.3 7.6 %collective-permute-start.22 = (bf16[128,256]{0,1:T(8,128)(2,1)S(1)}, bf16[128,256]{0,1:T(8,128)(2,1)S(1)}, u32[]{:S(2)}, u32[]{:S(2)}) collective-permute-start(bf16[128,256]{0,1:T(8,128)(2,1)S(1)} %get-tuple-element.15), channel_id=1, source_target_pairs={{0,1},{1,2},{2,3},{3,4},{4,5},{5,6},{6,7},{7,8},{8,9},{9,10},{10,1... | collective-permute-start | bytes 196616 | tf_op jit(solution)/shard_map/ppermute | solution.py:13
  348.3 11.4 %collective-permute-start.21 = (bf16[128,256]{0,1:T(8,128)(2,1)S(1)}, bf16[128,256]{0,1:T(8,128)(2,1)S(1)}, u32[]{:S(2)}, u32[]{:S(2)}) collective-permute-start(bf16[128,256]{0,1:T(8,128)(2,1)S(1)} %get-tuple-element.16), channel_id=1, source_target_pairs={{16,0},{32,16},{48,32},{64,48},{80,64},{96,80},{112,96},{128,112},... | collective-permute-start | bytes 196616 | tf_op jit(solution)/shard_map/ppermute | solution.py:13
  367.9 10.9 %collective-permute-start.24 = (bf16[128,256]{1,0:T(8,128)(2,1)S(1)}, bf16[128,256]{1,0:T(8,128)(2,1)S(1)}, u32[]{:S(2)}, u32[]{:S(2)}) collective-permute-start(bf16[128,256]{1,0:T(8,128)(2,1)S(1)} %get-tuple-element.29), channel_id=1, source_target_pairs={{0,16},{16,32},{32,48},{48,64},{64,80},{80,96},{96,112},{112,128},... | collective-permute-start | bytes 196616 | tf_op jit(solution)/shard_map/ppermute | solution.py:13
  369.8 9.0 %collective-permute-start.27 = (bf16[128,256]{1,0:T(8,128)(2,1)S(1)}, bf16[128,256]{1,0:T(8,128)(2,1)S(1)}, u32[]{:S(2)}, u32[]{:S(2)}) collective-permute-start(bf16[128,256]{1,0:T(8,128)(2,1)S(1)} %get-tuple-element.30), channel_id=1, source_target_pairs={{1,0},{2,1},{3,2},{4,3},{5,4},{6,5},{7,6},{8,7},{9,8},{10,9},{11,1... | collective-permute-start | bytes 196616 | tf_op jit(solution)/shard_map/ppermute | solution.py:13
  372.2 6.7 %collective-permute-start.26 = (bf16[128,256]{1,0:T(8,128)(2,1)S(1)}, bf16[128,256]{1,0:T(8,128)(2,1)S(1)}, u32[]{:S(2)}, u32[]{:S(2)}) collective-permute-start(bf16[128,256]{1,0:T(8,128)(2,1)S(1)} %get-tuple-element.31), channel_id=1, source_target_pairs={{0,1},{1,2},{2,3},{3,4},{4,5},{5,6},{6,7},{7,8},{8,9},{9,10},{10,1... | collective-permute-start | bytes 196616 | tf_op jit(solution)/shard_map/ppermute | solution.py:13
  375.4 11.0 %collective-permute-start.25 = (bf16[128,256]{1,0:T(8,128)(2,1)S(1)}, bf16[128,256]{1,0:T(8,128)(2,1)S(1)}, u32[]{:S(2)}, u32[]{:S(2)}) collective-permute-start(bf16[128,256]{1,0:T(8,128)(2,1)S(1)} %get-tuple-element.32), channel_id=1, source_target_pairs={{16,0},{32,16},{48,32},{64,48},{80,64},{96,80},{112,96},{128,112},... | collective-permute-start | bytes 196616 | tf_op jit(solution)/shard_map/ppermute | solution.py:13
  390.3 14.7 %collective-permute-start.28 = (bf16[128,256]{0,1:T(8,128)(2,1)S(1)}, bf16[128,256]{0,1:T(8,128)(2,1)S(1)}, u32[]{:S(2)}, u32[]{:S(2)}) collective-permute-start(bf16[128,256]{0,1:T(8,128)(2,1)S(1)} %get-tuple-element.9), channel_id=1, source_target_pairs={{0,16},{16,32},{32,48},{48,64},{64,80},{80,96},{96,112},{112,128},... | collective-permute-start | bytes 196616 | tf_op jit(solution)/shard_map/ppermute | solution.py:13
  392.4 12.6 %collective-permute-start.31 = (bf16[128,256]{0,1:T(8,128)(2,1)S(1)}, bf16[128,256]{0,1:T(8,128)(2,1)S(1)}, u32[]{:S(2)}, u32[]{:S(2)}) collective-permute-start(bf16[128,256]{0,1:T(8,128)(2,1)S(1)} %get-tuple-element.10), channel_id=1, source_target_pairs={{1,0},{2,1},{3,2},{4,3},{5,4},{6,5},{7,6},{8,7},{9,8},{10,9},{11,1... | collective-permute-start | bytes 196616 | tf_op jit(solution)/shard_map/ppermute | solution.py:13
  394.3 10.6 %collective-permute-start.30 = (bf16[128,256]{0,1:T(8,128)(2,1)S(1)}, bf16[128,256]{0,1:T(8,128)(2,1)S(1)}, u32[]{:S(2)}, u32[]{:S(2)}) collective-permute-start(bf16[128,256]{0,1:T(8,128)(2,1)S(1)} %get-tuple-element.11), channel_id=1, source_target_pairs={{0,1},{1,2},{2,3},{3,4},{4,5},{5,6},{6,7},{7,8},{8,9},{9,10},{10,1... | collective-permute-start | bytes 196616 | tf_op jit(solution)/shard_map/ppermute | solution.py:13
  398.0 9.4 %collective-permute-start.29 = (bf16[128,256]{0,1:T(8,128)(2,1)S(1)}, bf16[128,256]{0,1:T(8,128)(2,1)S(1)}, u32[]{:S(2)}, u32[]{:S(2)}) collective-permute-start(bf16[128,256]{0,1:T(8,128)(2,1)S(1)} %get-tuple-element.12), channel_id=1, source_target_pairs={{16,0},{32,16},{48,32},{64,48},{80,64},{96,80},{112,96},{128,112},... | collective-permute-start | bytes 196616 | tf_op jit(solution)/shard_map/ppermute | solution.py:13
  418.6 11.3 %collective-permute-start.32 = (bf16[128,256]{1,0:T(8,128)(2,1)S(1)}, bf16[128,256]{1,0:T(8,128)(2,1)S(1)}, u32[]{:S(2)}, u32[]{:S(2)}) collective-permute-start(bf16[128,256]{1,0:T(8,128)(2,1)S(1)} %get-tuple-element.25), channel_id=1, source_target_pairs={{0,16},{16,32},{32,48},{48,64},{64,80},{80,96},{96,112},{112,128},... | collective-permute-start | bytes 196616 | tf_op jit(solution)/shard_map/ppermute | solution.py:13
  422.4 7.5 %collective-permute-start.35 = (bf16[128,256]{1,0:T(8,128)(2,1)S(1)}, bf16[128,256]{1,0:T(8,128)(2,1)S(1)}, u32[]{:S(2)}, u32[]{:S(2)}) collective-permute-start(bf16[128,256]{1,0:T(8,128)(2,1)S(1)} %get-tuple-element.26), channel_id=1, source_target_pairs={{1,0},{2,1},{3,2},{4,3},{5,4},{6,5},{7,6},{8,7},{9,8},{10,9},{11,1... | collective-permute-start | bytes 196616 | tf_op jit(solution)/shard_map/ppermute | solution.py:13
  424.3 5.6 collective-permute-start.34
  428.0 9.9 %collective-permute-start.33 = (bf16[128,256]{1,0:T(8,128)(2,1)S(1)}, bf16[128,256]{1,0:T(8,128)(2,1)S(1)}, u32[]{:S(2)}, u32[]{:S(2)}) collective-permute-start(bf16[128,256]{1,0:T(8,128)(2,1)S(1)} %get-tuple-element.28), channel_id=1, source_target_pairs={{16,0},{32,16},{48,32},{64,48},{80,64},{96,80},{112,96},{128,112},... | collective-permute-start | bytes 196616 | tf_op jit(solution)/shard_map/ppermute | solution.py:13
  437.9 0.7 copy-start.2
  541.9 18.0 %collective-permute-start.36 = (bf16[128,256]{0,1:T(8,128)(2,1)S(1)}, bf16[128,256]{0,1:T(8,128)(2,1)S(1)}, u32[]{:S(2)}, u32[]{:S(2)}) collective-permute-start(bf16[128,256]{0,1:T(8,128)(2,1)S(1)} %get-tuple-element.5), channel_id=1, source_target_pairs={{0,16},{16,32},{32,48},{48,64},{64,80},{80,96},{96,112},{112,128},... | collective-permute-start | bytes 196616 | tf_op jit(solution)/shard_map/ppermute | solution.py:13
  546.4 13.5 %collective-permute-start.39 = (bf16[128,256]{0,1:T(8,128)(2,1)S(1)}, bf16[128,256]{0,1:T(8,128)(2,1)S(1)}, u32[]{:S(2)}, u32[]{:S(2)}) collective-permute-start(bf16[128,256]{0,1:T(8,128)(2,1)S(1)} %get-tuple-element.6), channel_id=1, source_target_pairs={{1,0},{2,1},{3,2},{4,3},{5,4},{6,5},{7,6},{8,7},{9,8},{10,9},{11,1... | collective-permute-start | bytes 196616 | tf_op jit(solution)/shard_map/ppermute | solution.py:13
  551.4 8.6 %collective-permute-start.38 = (bf16[128,256]{0,1:T(8,128)(2,1)S(1)}, bf16[128,256]{0,1:T(8,128)(2,1)S(1)}, u32[]{:S(2)}, u32[]{:S(2)}) collective-permute-start(bf16[128,256]{0,1:T(8,128)(2,1)S(1)} %get-tuple-element.7), channel_id=1, source_target_pairs={{0,1},{1,2},{2,3},{3,4},{4,5},{5,6},{6,7},{7,8},{8,9},{9,10},{10,1... | collective-permute-start | bytes 196616 | tf_op jit(solution)/shard_map/ppermute | solution.py:13
  554.4 11.2 %collective-permute-start.37 = (bf16[128,256]{0,1:T(8,128)(2,1)S(1)}, bf16[128,256]{0,1:T(8,128)(2,1)S(1)}, u32[]{:S(2)}, u32[]{:S(2)}) collective-permute-start(bf16[128,256]{0,1:T(8,128)(2,1)S(1)} %get-tuple-element.8), channel_id=1, source_target_pairs={{16,0},{32,16},{48,32},{64,48},{80,64},{96,80},{112,96},{128,112},... | collective-permute-start | bytes 196616 | tf_op jit(solution)/shard_map/ppermute | solution.py:13
Sparse Core Ops, SparseCore 0:
  54.3 79.2 reduce-scatter.9
  251.8 82.0 reduce-scatter.11
  457.8 82.2 reduce-scatter.13
where the time goes:
time: 584 us; the launch traced here: 582 us
  waiting for transfers between devices  296 us (51%)
  starting transfers between devices  123 us (21%)
  blocking collectives  54.9 us (9%)
  other arithmetic  36 us (6%)
  local copies, waits for them, and re-layouts  30.1 us (5%)
  matrix products  27.8 us (5%)
  between operations  14.1 us (2%)
    unnamed x6, waiting for transfers between devices  230 us
    ppermute x40, starting transfers between devices, passed_along(): return lax.ppermute(shard, axis, pairs)  123 us
    ppermute x40, waiting for transfers between devices, passed_along(): return lax.ppermute(shard, axis, pairs)  65.8 us
    all_gather x3, blocking collectives, per_device(): block_rows = lax.all_gather(restricted, 'col', axis=0, tiled=True)  54.9 us
    scatter-add x5, other arithmetic, owner_sum(): summed = jnp.zeros((own_rows, columns), jnp.float32).at[flat_rows].add(we...  21.8 us
    dot_general x3, matrix products, per_device(): jnp.dot(inverse, residual_local, preferred_element_type=jnp.float32)  13.8 us
    slice x10, local copies, waits for them, and re-layouts, owner_sum(): return local_terms[:own_rows] + summed  12.9 us
  transfers between devices with their start and end apart: 43, of which 13 were waited for; matrix products, arithmetic and copies ran while one was open for 5% of the time, Pallas kernels for 0%

commit v1 on v0

--- a/solution.py
+++ b/solution.py
@@ -72,7 +72,9 @@
             prolong, residual_local, (((0,), (0,)), ((), ())), preferred_element_type=jnp.float32
         )
         restricted = restricted.astype(jnp.bfloat16)
-        block_rows = lax.all_gather(restricted, "col", axis=0, tiled=True)
+        block_rows = jnp.concatenate(
+            lax.all_to_all(jnp.stack([restricted] * lax.axis_size("col")), "col", 0, 0), axis=0
+        )
         solved = lax.psum_scatter(
             jnp.dot(coarse_rows, block_rows, preferred_element_type=jnp.float32).astype(
                 jnp.bfloat16

time: 584 us -> 564 us (0.966)
  blocking collectives: 54.9 us -> 40.8 us
  waiting for transfers between devices: 296 us -> 290 us
    all_gather x3 -> x0, blocking collectives: 54.9 us -> none  [per_device(): block_rows = lax.all_gather(restricted, 'col', axis=0, tiled=True)]
    all_to_all x0 -> x3, blocking collectives: none -> 40.8 us  [per_device(): lax.all_to_all(jnp.stack([restricted] * lax.axis_size('col')), 'col', 0, 0)]
where the time goes in v1:
time: 564 us; the launch traced here: 562 us
  waiting for transfers between devices  290 us (51%)
  starting transfers between devices  123 us (22%)
  blocking collectives  40.8 us (7%)
  other arithmetic  36 us (6%)
  local copies, waits for them, and re-layouts  29.8 us (5%)
  matrix products  27.8 us (5%)
  between operations  14.1 us (2%)
    unnamed x6, waiting for transfers between devices  225 us
    ppermute x40, starting transfers between devices, passed_along(): return lax.ppermute(shard, axis, pairs)  123 us
    ppermute x40, waiting for transfers between devices, passed_along(): return lax.ppermute(shard, axis, pairs)  65 us
    all_to_all x3, blocking collectives, per_device(): lax.all_to_all(jnp.stack([restricted] * lax.axis_size('col')), 'col', 0, 0)  40.8 us
    scatter-add x5, other arithmetic, owner_sum(): summed = jnp.zeros((own_rows, columns), jnp.float32).at[flat_rows].add(we...  21.8 us
    dot_general x3, matrix products, per_device(): jnp.dot(inverse, residual_local, preferred_element_type=jnp.float32)  13.8 us
    slice x10, local copies, waits for them, and re-layouts, owner_sum(): return local_terms[:own_rows] + summed  12.9 us
  transfers between devices with their start and end apart: 43, of which 13 were waited for; matrix products, arithmetic and copies ran while one was open for 5% of the time, Pallas kernels for 0%

profile of v1, /device:TPU:89, one launch (start us, length us, event | category | flops | bytes accessed | tf_op | source)
XLA Modules:
  0.0 562.3 jit_solution(9247706597383473492)
XLA Ops:
  11.4 5.8 %collective-permute-start = (bf16[128,256]{1,0:T(8,128)(2,1)S(1)}, bf16[128,256]{1,0:T(8,128)(2,1)S(1)}, u32[]{:S(2)}, u32[]{:S(2)}) collective-permute-start(bf16[128,256]{1,0:T(8,128)(2,1)S(1)} %get-tuple-element.41), channel_id=1, source_target_pairs={{0,16},{16,32},{32,48},{48,64},{64,80},{80,96},{96,112},{112,128},... | collective-permute-start | bytes 196616 | tf_op jit(solution)/shard_map/ppermute | solution.py:13
  20.1 3.0 collective-permute-start.2
  25.1 8.6 %collective-permute-done.1 = bf16[128,256]{1,0:T(8,128)(2,1)S(1)} collective-permute-done((bf16[128,256]{1,0:T(8,128)(2,1)S(1)}, bf16[128,256]{1,0:T(8,128)(2,1)S(1)}, u32[]{:S(2)}, u32[]{:S(2)}) %collective-permute-start.1) | collective-permute-done | bytes 65568 | tf_op jit(solution)/shard_map/ppermute | solution.py:13
  34.0 12.5 %all_to_all.15 = bf16[16,32,256]{2,1,0:T(8,128)(2,1)S(1)} all-to-all(bf16[16,32,256]{2,1,0:T(8,128)(2,1)S(1)} %stack.212), channel_id=1, replica_groups=mesh['row'=16,'col'=16] {'col'}, dimensions={0} | all-to-all | bytes 524288 | tf_op jit(solution)/shard_map/all_to_all | solution.py:76
  47.7 3.8 fusion.8
  51.5 75.9 %reduce-scatter.10.cloned.1.call-done = bf16[32,256]{1,0:T(8,128)(2,1)} async-done(((bf16[512,256]{1,0:T(8,128)(2,1)}), bf16[32,256]{1,0:T(8,128)(2,1)}) %reduce-scatter.10.cloned.1.call-update) | async-done | bytes 16400
  128.6 4.3 collective-permute-start.4
  132.9 5.2 collective-permute-start.7
  138.1 3.0 collective-permute-start.6
  143.5 8.8 %collective-permute-done.5 = bf16[128,256]{0,1:T(8,128)(2,1)S(1)} collective-permute-done((bf16[128,256]{0,1:T(8,128)(2,1)S(1)}, bf16[128,256]{0,1:T(8,128)(2,1)S(1)}, u32[]{:S(2)}, u32[]{:S(2)}) %collective-permute-start.5) | collective-permute-done | bytes 65568 | tf_op jit(solution)/shard_map/ppermute | solution.py:13
  152.7 3.7 scatter_fusion
  162.5 3.6 collective-permute-start.10
  166.2 3.4 collective-permute-start.9
  169.6 7.2 %collective-permute-done.9 = bf16[128,256]{1,0:T(8,128)(2,1)S(1)} collective-permute-done((bf16[128,256]{1,0:T(8,128)(2,1)S(1)}, bf16[128,256]{1,0:T(8,128)(2,1)S(1)}, u32[]{:S(2)}, u32[]{:S(2)}) %collective-permute-start.9) | collective-permute-done | bytes 65568 | tf_op jit(solution)/shard_map/ppermute | solution.py:13
  176.8 3.8 fusion.54
  184.5 3.6 collective-permute-start.14
  188.2 3.4 collective-permute-start.13
  194.2 3.5 collective-permute-done.13
  200.0 3.9 scatter_fusion.1
  211.9 3.6 collective-permute-start.18
  215.6 3.5 collective-permute-start.17
  219.1 6.4 %collective-permute-done.17 = bf16[128,256]{1,0:T(8,128)(2,1)S(1)} collective-permute-done((bf16[128,256]{1,0:T(8,128)(2,1)S(1)}, bf16[128,256]{1,0:T(8,128)(2,1)S(1)}, u32[]{:S(2)}, u32[]{:S(2)}) %collective-permute-start.17) | collective-permute-done | bytes 65568 | tf_op jit(solution)/shard_map/ppermute | solution.py:13
  225.8 14.0 %all_to_all.16 = bf16[16,32,256]{2,1,0:T(8,128)(2,1)S(1)} all-to-all(bf16[16,32,256]{2,1,0:T(8,128)(2,1)S(1)} %stack.233), channel_id=1, replica_groups=mesh['row'=16,'col'=16] {'col'}, dimensions={0} | all-to-all | bytes 524288 | tf_op jit(solution)/shard_map/all_to_all | solution.py:76
  241.1 5.0 fusion.6
  246.0 74.8 %reduce-scatter.12.cloned.1.call-done = bf16[32,256]{1,0:T(8,128)(2,1)} async-done(((bf16[512,256]{1,0:T(8,128)(2,1)}), bf16[32,256]{1,0:T(8,128)(2,1)}) %reduce-scatter.12.cloned.1.call-update) | async-done | bytes 16400
  322.7 4.5 collective-permute-start.20
  327.3 4.9 collective-permute-start.23
  332.2 3.0 collective-permute-start.22
  339.8 6.8 %collective-permute-done.21 = bf16[128,256]{0,1:T(8,128)(2,1)S(1)} collective-permute-done((bf16[128,256]{0,1:T(8,128)(2,1)S(1)}, bf16[128,256]{0,1:T(8,128)(2,1)S(1)}, u32[]{:S(2)}, u32[]{:S(2)}) %collective-permute-start.21) | collective-permute-done | bytes 65568 | tf_op jit(solution)/shard_map/ppermute | solution.py:13
  348.8 3.7 scatter_fusion.2
  359.1 3.3 collective-permute-start.26
  362.4 3.6 collective-permute-start.25
  366.0 7.3 %collective-permute-done.25 = bf16[128,256]{1,0:T(8,128)(2,1)S(1)} collective-permute-done((bf16[128,256]{1,0:T(8,128)(2,1)S(1)}, bf16[128,256]{1,0:T(8,128)(2,1)S(1)}, u32[]{:S(2)}, u32[]{:S(2)}) %collective-permute-start.25) | collective-permute-done | bytes 65568 | tf_op jit(solution)/shard_map/ppermute | solution.py:13
  373.4 3.8 fusion.56
  381.1 3.6 collective-permute-start.30
  384.7 3.4 collective-permute-start.29
  396.4 5.2 scatter_fusion.3
  405.4 3.7 collective-permute-start.32
  411.0 3.6 collective-permute-start.34
  416.8 7.8 %collective-permute-done.33 = bf16[128,256]{1,0:T(8,128)(2,1)S(1)} collective-permute-done((bf16[128,256]{1,0:T(8,128)(2,1)S(1)}, bf16[128,256]{1,0:T(8,128)(2,1)S(1)}, u32[]{:S(2)}, u32[]{:S(2)}) %collective-permute-start.33) | collective-permute-done | bytes 65568 | tf_op jit(solution)/shard_map/ppermute | solution.py:13
  424.9 14.3 %all_to_all.17 = bf16[16,32,256]{2,1,0:T(8,128)(2,1)S(1)} all-to-all(bf16[16,32,256]{2,1,0:T(8,128)(2,1)S(1)} %stack.254), channel_id=1, replica_groups=mesh['row'=16,'col'=16] {'col'}, dimensions={0} | all-to-all | bytes 524288 | tf_op jit(solution)/shard_map/all_to_all | solution.py:76
  440.4 5.0 fusion.4
  445.5 74.7 %reduce-scatter.14.cloned.1.call-done = bf16[32,256]{1,0:T(8,128)(2,1)} async-done(((bf16[512,256]{1,0:T(8,128)(2,1)}), bf16[32,256]{1,0:T(8,128)(2,1)}) %reduce-scatter.14.cloned.1.call-update) | async-done | bytes 16400
  522.0 4.5 collective-permute-start.36
  526.5 5.0 collective-permute-start.39
  531.5 3.0 collective-permute-start.38
  540.1 5.9 %collective-permute-done.37 = bf16[128,256]{0,1:T(8,128)(2,1)S(1)} collective-permute-done((bf16[128,256]{0,1:T(8,128)(2,1)S(1)}, bf16[128,256]{0,1:T(8,128)(2,1)S(1)}, u32[]{:S(2)}, u32[]{:S(2)}) %collective-permute-start.37) | collective-permute-done | bytes 65568 | tf_op jit(solution)/shard_map/ppermute | solution.py:13
  548.2 5.2 scatter_fusion.4
  (134 shorter events, 88.1 us)
Async XLA Ops:
  6.5 39.9 %copy-start = (bf16[16,32,512]{2,1,0:T(8,128)(2,1)S(1)}, bf16[16,32,512]{2,1,0:T(8,128)(2,1)}, u32[]{:S(2)}) copy-start(bf16[16,32,512]{2,1,0:T(8,128)(2,1)} %param.11) | copy-start | bytes 1572868
  6.5 120.9 %reduce-scatter.10.cloned.1.call-start = ((), (), s32[]{:S(2)}) async-start(), calls=%async_computation.6 | async-start | bytes 278528
  9.3 24.4 %copy-start.1 = (bf16[1,1,1536,32]{2,3,1,0:T(8,128)(2,1)S(1)}, bf16[1,1,1536,32]{2,3,1,0:T(8,128)(2,1)}, u32[]{:S(2)}) copy-start(bf16[1,1,1536,32]{2,3,1,0:T(8,128)(2,1)} %param.10) | copy-start | bytes 294916
  11.4 13.6 %collective-permute-start = (bf16[128,256]{1,0:T(8,128)(2,1)S(1)}, bf16[128,256]{1,0:T(8,128)(2,1)S(1)}, u32[]{:S(2)}, u32[]{:S(2)}) collective-permute-start(bf16[128,256]{1,0:T(8,128)(2,1)S(1)} %get-tuple-element.41), channel_id=1, source_target_pairs={{0,16},{16,32},{32,48},{48,64},{64,80},{80,96},{96,112},{112,128},... | collective-permute-start | bytes 196616 | tf_op jit(solution)/shard_map/ppermute | solution.py:13
  17.2 7.8 %collective-permute-start.3 = (bf16[128,256]{1,0:T(8,128)(2,1)S(1)}, bf16[128,256]{1,0:T(8,128)(2,1)S(1)}, u32[]{:S(2)}, u32[]{:S(2)}) collective-permute-start(bf16[128,256]{1,0:T(8,128)(2,1)S(1)} %get-tuple-element.42), channel_id=1, source_target_pairs={{1,0},{2,1},{3,2},{4,3},{5,4},{6,5},{7,6},{8,7},{9,8},{10,9},{11,1... | collective-permute-start | bytes 196616 | tf_op jit(solution)/shard_map/ppermute | solution.py:13
  20.1 5.0 collective-permute-start.2
  23.1 10.5 %collective-permute-start.1 = (bf16[128,256]{1,0:T(8,128)(2,1)S(1)}, bf16[128,256]{1,0:T(8,128)(2,1)S(1)}, u32[]{:S(2)}, u32[]{:S(2)}) collective-permute-start(bf16[128,256]{1,0:T(8,128)(2,1)S(1)} %get-tuple-element.44), channel_id=1, source_target_pairs={{16,0},{32,16},{48,32},{64,48},{80,64},{96,80},{112,96},{128,112},... | collective-permute-start | bytes 196616 | tf_op jit(solution)/shard_map/ppermute | solution.py:13
  47.7 273.2 %reduce-scatter.12.cloned.1.call-start = ((), (), s32[]{:S(2)}) async-start(), calls=%async_computation.7 | async-start | bytes 278528
  128.6 14.8 %collective-permute-start.4 = (bf16[128,256]{0,1:T(8,128)(2,1)S(1)}, bf16[128,256]{0,1:T(8,128)(2,1)S(1)}, u32[]{:S(2)}, u32[]{:S(2)}) collective-permute-start(bf16[128,256]{0,1:T(8,128)(2,1)S(1)} %get-tuple-element.21), channel_id=1, source_target_pairs={{0,16},{16,32},{32,48},{48,64},{64,80},{80,96},{96,112},{112,128},... | collective-permute-start | bytes 196616 | tf_op jit(solution)/shard_map/ppermute | solution.py:13
  132.9 10.5 %collective-permute-start.7 = (bf16[128,256]{0,1:T(8,128)(2,1)S(1)}, bf16[128,256]{0,1:T(8,128)(2,1)S(1)}, u32[]{:S(2)}, u32[]{:S(2)}) collective-permute-start(bf16[128,256]{0,1:T(8,128)(2,1)S(1)} %get-tuple-element.22), channel_id=1, source_target_pairs={{1,0},{2,1},{3,2},{4,3},{5,4},{6,5},{7,6},{8,7},{9,8},{10,9},{11,1... | collective-permute-start | bytes 196616 | tf_op jit(solution)/shard_map/ppermute | solution.py:13
  138.1 5.4 collective-permute-start.6
  141.1 11.2 %collective-permute-start.5 = (bf16[128,256]{0,1:T(8,128)(2,1)S(1)}, bf16[128,256]{0,1:T(8,128)(2,1)S(1)}, u32[]{:S(2)}, u32[]{:S(2)}) collective-permute-start(bf16[128,256]{0,1:T(8,128)(2,1)S(1)} %get-tuple-element.24), channel_id=1, source_target_pairs={{16,0},{32,16},{48,32},{64,48},{80,64},{96,80},{112,96},{128,112},... | collective-permute-start | bytes 196616 | tf_op jit(solution)/shard_map/ppermute | solution.py:13
  158.6 10.9 %collective-permute-start.8 = (bf16[128,256]{1,0:T(8,128)(2,1)S(1)}, bf16[128,256]{1,0:T(8,128)(2,1)S(1)}, u32[]{:S(2)}, u32[]{:S(2)}) collective-permute-start(bf16[128,256]{1,0:T(8,128)(2,1)S(1)} %get-tuple-element.37), channel_id=1, source_target_pairs={{0,16},{16,32},{32,48},{48,64},{64,80},{80,96},{96,112},{112,128},... | collective-permute-start | bytes 196616 | tf_op jit(solution)/shard_map/ppermute | solution.py:13
  160.6 9.0 %collective-permute-start.11 = (bf16[128,256]{1,0:T(8,128)(2,1)S(1)}, bf16[128,256]{1,0:T(8,128)(2,1)S(1)}, u32[]{:S(2)}, u32[]{:S(2)}) collective-permute-start(bf16[128,256]{1,0:T(8,128)(2,1)S(1)} %get-tuple-element.38), channel_id=1, source_target_pairs={{1,0},{2,1},{3,2},{4,3},{5,4},{6,5},{7,6},{8,7},{9,8},{10,9},{11,1... | collective-permute-start | bytes 196616 | tf_op jit(solution)/shard_map/ppermute | solution.py:13
  162.5 7.0 %collective-permute-start.10 = (bf16[128,256]{1,0:T(8,128)(2,1)S(1)}, bf16[128,256]{1,0:T(8,128)(2,1)S(1)}, u32[]{:S(2)}, u32[]{:S(2)}) collective-permute-start(bf16[128,256]{1,0:T(8,128)(2,1)S(1)} %get-tuple-element.39), channel_id=1, source_target_pairs={{0,1},{1,2},{2,3},{3,4},{4,5},{5,6},{6,7},{7,8},{8,9},{9,10},{10,1... | collective-permute-start | bytes 196616 | tf_op jit(solution)/shard_map/ppermute | solution.py:13
  166.2 10.6 %collective-permute-start.9 = (bf16[128,256]{1,0:T(8,128)(2,1)S(1)}, bf16[128,256]{1,0:T(8,128)(2,1)S(1)}, u32[]{:S(2)}, u32[]{:S(2)}) collective-permute-start(bf16[128,256]{1,0:T(8,128)(2,1)S(1)} %get-tuple-element.40), channel_id=1, source_target_pairs={{16,0},{32,16},{48,32},{64,48},{80,64},{96,80},{112,96},{128,112},... | collective-permute-start | bytes 196616 | tf_op jit(solution)/shard_map/ppermute | solution.py:13
  180.7 13.5 %collective-permute-start.12 = (bf16[128,256]{0,1:T(8,128)(2,1)S(1)}, bf16[128,256]{0,1:T(8,128)(2,1)S(1)}, u32[]{:S(2)}, u32[]{:S(2)}) collective-permute-start(bf16[128,256]{0,1:T(8,128)(2,1)S(1)} %get-tuple-element.17), channel_id=1, source_target_pairs={{0,16},{16,32},{32,48},{48,64},{64,80},{80,96},{96,112},{112,128},... | collective-permute-start | bytes 196616 | tf_op jit(solution)/shard_map/ppermute | solution.py:13
  182.6 11.6 %collective-permute-start.15 = (bf16[128,256]{0,1:T(8,128)(2,1)S(1)}, bf16[128,256]{0,1:T(8,128)(2,1)S(1)}, u32[]{:S(2)}, u32[]{:S(2)}) collective-permute-start(bf16[128,256]{0,1:T(8,128)(2,1)S(1)} %get-tuple-element.18), channel_id=1, source_target_pairs={{1,0},{2,1},{3,2},{4,3},{5,4},{6,5},{7,6},{8,7},{9,8},{10,9},{11,1... | collective-permute-start | bytes 196616 | tf_op jit(solution)/shard_map/ppermute | solution.py:13
  184.5 9.7 %collective-permute-start.14 = (bf16[128,256]{0,1:T(8,128)(2,1)S(1)}, bf16[128,256]{0,1:T(8,128)(2,1)S(1)}, u32[]{:S(2)}, u32[]{:S(2)}) collective-permute-start(bf16[128,256]{0,1:T(8,128)(2,1)S(1)} %get-tuple-element.19), channel_id=1, source_target_pairs={{0,1},{1,2},{2,3},{3,4},{4,5},{5,6},{6,7},{7,8},{8,9},{9,10},{10,1... | collective-permute-start | bytes 196616 | tf_op jit(solution)/shard_map/ppermute | solution.py:13
  188.2 9.6 %collective-permute-start.13 = (bf16[128,256]{0,1:T(8,128)(2,1)S(1)}, bf16[128,256]{0,1:T(8,128)(2,1)S(1)}, u32[]{:S(2)}, u32[]{:S(2)}) collective-permute-start(bf16[128,256]{0,1:T(8,128)(2,1)S(1)} %get-tuple-element.20), channel_id=1, source_target_pairs={{16,0},{32,16},{48,32},{64,48},{80,64},{96,80},{112,96},{128,112},... | collective-permute-start | bytes 196616 | tf_op jit(solution)/shard_map/ppermute | solution.py:13
  207.4 11.7 %collective-permute-start.16 = (bf16[128,256]{1,0:T(8,128)(2,1)S(1)}, bf16[128,256]{1,0:T(8,128)(2,1)S(1)}, u32[]{:S(2)}, u32[]{:S(2)}) collective-permute-start(bf16[128,256]{1,0:T(8,128)(2,1)S(1)} %get-tuple-element.33), channel_id=1, source_target_pairs={{0,16},{16,32},{32,48},{48,64},{64,80},{80,96},{96,112},{112,128},... | collective-permute-start | bytes 196616 | tf_op jit(solution)/shard_map/ppermute | solution.py:13
  210.0 9.1 %collective-permute-start.19 = (bf16[128,256]{1,0:T(8,128)(2,1)S(1)}, bf16[128,256]{1,0:T(8,128)(2,1)S(1)}, u32[]{:S(2)}, u32[]{:S(2)}) collective-permute-start(bf16[128,256]{1,0:T(8,128)(2,1)S(1)} %get-tuple-element.34), channel_id=1, source_target_pairs={{1,0},{2,1},{3,2},{4,3},{5,4},{6,5},{7,6},{8,7},{9,8},{10,9},{11,1... | collective-permute-start | bytes 196616 | tf_op jit(solution)/shard_map/ppermute | solution.py:13
  211.9 7.2 %collective-permute-start.18 = (bf16[128,256]{1,0:T(8,128)(2,1)S(1)}, bf16[128,256]{1,0:T(8,128)(2,1)S(1)}, u32[]{:S(2)}, u32[]{:S(2)}) collective-permute-start(bf16[128,256]{1,0:T(8,128)(2,1)S(1)} %get-tuple-element.35), channel_id=1, source_target_pairs={{0,1},{1,2},{2,3},{3,4},{4,5},{5,6},{6,7},{7,8},{8,9},{9,10},{10,1... | collective-permute-start | bytes 196616 | tf_op jit(solution)/shard_map/ppermute | solution.py:13
  215.6 9.9 %collective-permute-start.17 = (bf16[128,256]{1,0:T(8,128)(2,1)S(1)}, bf16[128,256]{1,0:T(8,128)(2,1)S(1)}, u32[]{:S(2)}, u32[]{:S(2)}) collective-permute-start(bf16[128,256]{1,0:T(8,128)(2,1)S(1)} %get-tuple-element.36), channel_id=1, source_target_pairs={{16,0},{32,16},{48,32},{64,48},{80,64},{96,80},{112,96},{128,112},... | collective-permute-start | bytes 196616 | tf_op jit(solution)/shard_map/ppermute | solution.py:13
  241.0 279.1 %reduce-scatter.14.cloned.1.call-start = ((), (), s32[]{:S(2)}) async-start(), calls=%async_computation.8 | async-start | bytes 278528
  322.7 17.0 %collective-permute-start.20 = (bf16[128,256]{0,1:T(8,128)(2,1)S(1)}, bf16[128,256]{0,1:T(8,128)(2,1)S(1)}, u32[]{:S(2)}, u32[]{:S(2)}) collective-permute-start(bf16[128,256]{0,1:T(8,128)(2,1)S(1)} %get-tuple-element.13), channel_id=1, source_target_pairs={{0,16},{16,32},{32,48},{48,64},{64,80},{80,96},{96,112},{112,128},... | collective-permute-start | bytes 196616 | tf_op jit(solution)/shard_map/ppermute | solution.py:13
  327.3 12.5 %collective-permute-start.23 = (bf16[128,256]{0,1:T(8,128)(2,1)S(1)}, bf16[128,256]{0,1:T(8,128)(2,1)S(1)}, u32[]{:S(2)}, u32[]{:S(2)}) collective-permute-start(bf16[128,256]{0,1:T(8,128)(2,1)S(1)} %get-tuple-element.14), channel_id=1, source_target_pairs={{1,0},{2,1},{3,2},{4,3},{5,4},{6,5},{7,6},{8,7},{9,8},{10,9},{11,1... | collective-permute-start | bytes 196616 | tf_op jit(solution)/shard_map/ppermute | solution.py:13
  332.2 7.6 %collective-permute-start.22 = (bf16[128,256]{0,1:T(8,128)(2,1)S(1)}, bf16[128,256]{0,1:T(8,128)(2,1)S(1)}, u32[]{:S(2)}, u32[]{:S(2)}) collective-permute-start(bf16[128,256]{0,1:T(8,128)(2,1)S(1)} %get-tuple-element.15), channel_id=1, source_target_pairs={{0,1},{1,2},{2,3},{3,4},{4,5},{5,6},{6,7},{7,8},{8,9},{9,10},{10,1... | collective-permute-start | bytes 196616 | tf_op jit(solution)/shard_map/ppermute | solution.py:13
  335.2 11.4 %collective-permute-start.21 = (bf16[128,256]{0,1:T(8,128)(2,1)S(1)}, bf16[128,256]{0,1:T(8,128)(2,1)S(1)}, u32[]{:S(2)}, u32[]{:S(2)}) collective-permute-start(bf16[128,256]{0,1:T(8,128)(2,1)S(1)} %get-tuple-element.16), channel_id=1, source_target_pairs={{16,0},{32,16},{48,32},{64,48},{80,64},{96,80},{112,96},{128,112},... | collective-permute-start | bytes 196616 | tf_op jit(solution)/shard_map/ppermute | solution.py:13
  354.9 11.1 %collective-permute-start.24 = (bf16[128,256]{1,0:T(8,128)(2,1)S(1)}, bf16[128,256]{1,0:T(8,128)(2,1)S(1)}, u32[]{:S(2)}, u32[]{:S(2)}) collective-permute-start(bf16[128,256]{1,0:T(8,128)(2,1)S(1)} %get-tuple-element.29), channel_id=1, source_target_pairs={{0,16},{16,32},{32,48},{48,64},{64,80},{80,96},{96,112},{112,128},... | collective-permute-start | bytes 196616 | tf_op jit(solution)/shard_map/ppermute | solution.py:13
  356.8 9.2 %collective-permute-start.27 = (bf16[128,256]{1,0:T(8,128)(2,1)S(1)}, bf16[128,256]{1,0:T(8,128)(2,1)S(1)}, u32[]{:S(2)}, u32[]{:S(2)}) collective-permute-start(bf16[128,256]{1,0:T(8,128)(2,1)S(1)} %get-tuple-element.30), channel_id=1, source_target_pairs={{1,0},{2,1},{3,2},{4,3},{5,4},{6,5},{7,6},{8,7},{9,8},{10,9},{11,1... | collective-permute-start | bytes 196616 | tf_op jit(solution)/shard_map/ppermute | solution.py:13
  359.1 6.9 %collective-permute-start.26 = (bf16[128,256]{1,0:T(8,128)(2,1)S(1)}, bf16[128,256]{1,0:T(8,128)(2,1)S(1)}, u32[]{:S(2)}, u32[]{:S(2)}) collective-permute-start(bf16[128,256]{1,0:T(8,128)(2,1)S(1)} %get-tuple-element.31), channel_id=1, source_target_pairs={{0,1},{1,2},{2,3},{3,4},{4,5},{5,6},{6,7},{7,8},{8,9},{9,10},{10,1... | collective-permute-start | bytes 196616 | tf_op jit(solution)/shard_map/ppermute | solution.py:13
  362.4 11.0 %collective-permute-start.25 = (bf16[128,256]{1,0:T(8,128)(2,1)S(1)}, bf16[128,256]{1,0:T(8,128)(2,1)S(1)}, u32[]{:S(2)}, u32[]{:S(2)}) collective-permute-start(bf16[128,256]{1,0:T(8,128)(2,1)S(1)} %get-tuple-element.32), channel_id=1, source_target_pairs={{16,0},{32,16},{48,32},{64,48},{80,64},{96,80},{112,96},{128,112},... | collective-permute-start | bytes 196616 | tf_op jit(solution)/shard_map/ppermute | solution.py:13
  377.2 14.5 %collective-permute-start.28 = (bf16[128,256]{0,1:T(8,128)(2,1)S(1)}, bf16[128,256]{0,1:T(8,128)(2,1)S(1)}, u32[]{:S(2)}, u32[]{:S(2)}) collective-permute-start(bf16[128,256]{0,1:T(8,128)(2,1)S(1)} %get-tuple-element.9), channel_id=1, source_target_pairs={{0,16},{16,32},{32,48},{48,64},{64,80},{80,96},{96,112},{112,128},... | collective-permute-start | bytes 196616 | tf_op jit(solution)/shard_map/ppermute | solution.py:13
  379.1 12.6 %collective-permute-start.31 = (bf16[128,256]{0,1:T(8,128)(2,1)S(1)}, bf16[128,256]{0,1:T(8,128)(2,1)S(1)}, u32[]{:S(2)}, u32[]{:S(2)}) collective-permute-start(bf16[128,256]{0,1:T(8,128)(2,1)S(1)} %get-tuple-element.10), channel_id=1, source_target_pairs={{1,0},{2,1},{3,2},{4,3},{5,4},{6,5},{7,6},{8,7},{9,8},{10,9},{11,1... | collective-permute-start | bytes 196616 | tf_op jit(solution)/shard_map/ppermute | solution.py:13
  381.1 10.6 %collective-permute-start.30 = (bf16[128,256]{0,1:T(8,128)(2,1)S(1)}, bf16[128,256]{0,1:T(8,128)(2,1)S(1)}, u32[]{:S(2)}, u32[]{:S(2)}) collective-permute-start(bf16[128,256]{0,1:T(8,128)(2,1)S(1)} %get-tuple-element.11), channel_id=1, source_target_pairs={{0,1},{1,2},{2,3},{3,4},{4,5},{5,6},{6,7},{7,8},{8,9},{9,10},{10,1... | collective-permute-start | bytes 196616 | tf_op jit(solution)/shard_map/ppermute | solution.py:13
  384.7 9.5 %collective-permute-start.29 = (bf16[128,256]{0,1:T(8,128)(2,1)S(1)}, bf16[128,256]{0,1:T(8,128)(2,1)S(1)}, u32[]{:S(2)}, u32[]{:S(2)}) collective-permute-start(bf16[128,256]{0,1:T(8,128)(2,1)S(1)} %get-tuple-element.12), channel_id=1, source_target_pairs={{16,0},{32,16},{48,32},{64,48},{80,64},{96,80},{112,96},{128,112},... | collective-permute-start | bytes 196616 | tf_op jit(solution)/shard_map/ppermute | solution.py:13
  405.4 11.3 %collective-permute-start.32 = (bf16[128,256]{1,0:T(8,128)(2,1)S(1)}, bf16[128,256]{1,0:T(8,128)(2,1)S(1)}, u32[]{:S(2)}, u32[]{:S(2)}) collective-permute-start(bf16[128,256]{1,0:T(8,128)(2,1)S(1)} %get-tuple-element.25), channel_id=1, source_target_pairs={{0,16},{16,32},{32,48},{48,64},{64,80},{80,96},{96,112},{112,128},... | collective-permute-start | bytes 196616 | tf_op jit(solution)/shard_map/ppermute | solution.py:13
  409.1 7.7 %collective-permute-start.35 = (bf16[128,256]{1,0:T(8,128)(2,1)S(1)}, bf16[128,256]{1,0:T(8,128)(2,1)S(1)}, u32[]{:S(2)}, u32[]{:S(2)}) collective-permute-start(bf16[128,256]{1,0:T(8,128)(2,1)S(1)} %get-tuple-element.26), channel_id=1, source_target_pairs={{1,0},{2,1},{3,2},{4,3},{5,4},{6,5},{7,6},{8,7},{9,8},{10,9},{11,1... | collective-permute-start | bytes 196616 | tf_op jit(solution)/shard_map/ppermute | solution.py:13
  411.0 5.8 %collective-permute-start.34 = (bf16[128,256]{1,0:T(8,128)(2,1)S(1)}, bf16[128,256]{1,0:T(8,128)(2,1)S(1)}, u32[]{:S(2)}, u32[]{:S(2)}) collective-permute-start(bf16[128,256]{1,0:T(8,128)(2,1)S(1)} %get-tuple-element.27), channel_id=1, source_target_pairs={{0,1},{1,2},{2,3},{3,4},{4,5},{5,6},{6,7},{7,8},{8,9},{9,10},{10,1... | collective-permute-start | bytes 196616 | tf_op jit(solution)/shard_map/ppermute | solution.py:13
  414.7 9.9 %collective-permute-start.33 = (bf16[128,256]{1,0:T(8,128)(2,1)S(1)}, bf16[128,256]{1,0:T(8,128)(2,1)S(1)}, u32[]{:S(2)}, u32[]{:S(2)}) collective-permute-start(bf16[128,256]{1,0:T(8,128)(2,1)S(1)} %get-tuple-element.28), channel_id=1, source_target_pairs={{16,0},{32,16},{48,32},{64,48},{80,64},{96,80},{112,96},{128,112},... | collective-permute-start | bytes 196616 | tf_op jit(solution)/shard_map/ppermute | solution.py:13
  424.6 14.6 %copy-start.2 = (bf16[4,128,256]{2,1,0:T(8,128)(2,1)}, bf16[4,128,256]{2,1,0:T(8,128)(2,1)S(1)}, u32[]{:S(2)}) copy-start(bf16[4,128,256]{2,1,0:T(8,128)(2,1)S(1)} %pad_maximum_fusion.13) | copy-start | bytes 786436
  522.0 18.0 %collective-permute-start.36 = (bf16[128,256]{0,1:T(8,128)(2,1)S(1)}, bf16[128,256]{0,1:T(8,128)(2,1)S(1)}, u32[]{:S(2)}, u32[]{:S(2)}) collective-permute-start(bf16[128,256]{0,1:T(8,128)(2,1)S(1)} %get-tuple-element.5), channel_id=1, source_target_pairs={{0,16},{16,32},{32,48},{48,64},{64,80},{80,96},{96,112},{112,128},... | collective-permute-start | bytes 196616 | tf_op jit(solution)/shard_map/ppermute | solution.py:13
  526.5 13.5 %collective-permute-start.39 = (bf16[128,256]{0,1:T(8,128)(2,1)S(1)}, bf16[128,256]{0,1:T(8,128)(2,1)S(1)}, u32[]{:S(2)}, u32[]{:S(2)}) collective-permute-start(bf16[128,256]{0,1:T(8,128)(2,1)S(1)} %get-tuple-element.6), channel_id=1, source_target_pairs={{1,0},{2,1},{3,2},{4,3},{5,4},{6,5},{7,6},{8,7},{9,8},{10,9},{11,1... | collective-permute-start | bytes 196616 | tf_op jit(solution)/shard_map/ppermute | solution.py:13
  531.5 8.5 %collective-permute-start.38 = (bf16[128,256]{0,1:T(8,128)(2,1)S(1)}, bf16[128,256]{0,1:T(8,128)(2,1)S(1)}, u32[]{:S(2)}, u32[]{:S(2)}) collective-permute-start(bf16[128,256]{0,1:T(8,128)(2,1)S(1)} %get-tuple-element.7), channel_id=1, source_target_pairs={{0,1},{1,2},{2,3},{3,4},{4,5},{5,6},{6,7},{7,8},{8,9},{9,10},{10,1... | collective-permute-start | bytes 196616 | tf_op jit(solution)/shard_map/ppermute | solution.py:13
  534.5 11.4 %collective-permute-start.37 = (bf16[128,256]{0,1:T(8,128)(2,1)S(1)}, bf16[128,256]{0,1:T(8,128)(2,1)S(1)}, u32[]{:S(2)}, u32[]{:S(2)}) collective-permute-start(bf16[128,256]{0,1:T(8,128)(2,1)S(1)} %get-tuple-element.8), channel_id=1, source_target_pairs={{16,0},{32,16},{48,32},{64,48},{80,64},{96,80},{112,96},{128,112},... | collective-permute-start | bytes 196616 | tf_op jit(solution)/shard_map/ppermute | solution.py:13
Sparse Core Ops, SparseCore 0:
  47.8 79.5 reduce-scatter.9
  241.2 79.6 reduce-scatter.11
  440.5 79.5 reduce-scatter.13
